TPU v7x, 32 devices: a whole 2x2x4 slice. The times are simulated.
32 devices in a mesh: path: 8 (over z, core), fsdp: 4 (over y, x).
Axes of the slice: x: 2, y: 2, z: 4, core: 2. Of those that a mesh axis runs over, the one named last changes fastest.
Arguments:
- path_delta: bfloat16 [8, 4, 128, 4096], P('path', None, 'fsdp'), may hold values from -20 to 20
- feedback: float32 [8, 4, 128, 4096], P('path', None, 'fsdp'), may hold values from -4 to 4
- global_params: float32 [4, 2, 128, 4096], P(None, None, 'fsdp', 'path'), may hold values from -0.09375 to 0.09375
- momentum: float32 [4, 2, 128, 4096], P(None, None, 'fsdp', 'path'), may hold values from -2 to 2
- routes: int32 [8, 4], replicated, may hold values from 0 to 1
- token_counts: int32 [8, 4], replicated, may hold values from 1 to 16
- skip_flags: int32 [4, 2], replicated, may hold values from 0 to 1, as said below
Outputs:
- feedback_next: float32 [8, 4, 128, 4096], P('path', None, 'fsdp')
- momentum_next: float32 [4, 2, 128, 4096], P(None, None, 'fsdp', 'path')
- params_next: float32 [4, 2, 128, 4096], P(None, None, 'fsdp', 'path')
- path_params: bfloat16 [8, 4, 128, 4096], P('path', None, 'fsdp')
Inputs may be any that keep to these rules, and one draw needn't show every extreme that they name: `skip_flags`: at most one of the two modules of a level skips.
All inputs are finite; a program needn't handle non-finite values.
Results may differ from a plain program's by a relative error of at most 0.012.
Values may be sent and summed in bfloat16 or wider, within the bound.
A program may use at most 64 MiB of HBM per device.

v0:
```python
import jax
import jax.numpy as jnp
from jax import lax
from jax.sharding import PartitionSpec as P

clip_rms = 0.2
outer_rate = 0.7
momentum_coef = 0.9
epsilon_sq = 1e-06


def on_device(path_delta, feedback, global_params, momentum, routes, token_counts, skip_flags):
    own_index = lax.axis_index("path")
    counts = token_counts.astype(jnp.float32)
    same = (routes[:, None, :] == routes[None, :, :]).astype(jnp.float32)
    denom = jnp.sum(same * counts[None, :, :], axis=1)
    weight = counts / denom
    skipped_path = jnp.where(routes == 1, skip_flags[None, :, 1], skip_flags[None, :, 0])
    live = (1 - skipped_path).astype(jnp.float32)
    own_weight = lax.dynamic_slice_in_dim(weight, own_index, 1, 0)[0]
    own_live = lax.dynamic_slice_in_dim(live, own_index, 1, 0)[0]
    own_route = lax.dynamic_slice_in_dim(routes, own_index, 1, 0)[0]
    corrected = path_delta[0].astype(jnp.float32) + feedback[0]
    scaled = (own_weight[:, None, None] * corrected).astype(jnp.bfloat16)
    sent = jnp.where(own_live[:, None, None] > 0, scaled, jnp.zeros_like(scaled))
    feedback_next = corrected - own_live[:, None, None] * (
        sent.astype(jnp.float32) / own_weight[:, None, None]
    )
    own_hot = (own_route[:, None] == jnp.arange(2, dtype=jnp.int32)[None, :]).astype(jnp.float32)
    terms = own_hot[:, :, None, None] * sent.astype(jnp.float32)[:, None]
    average = lax.psum_scatter(
        terms.astype(jnp.bfloat16), "path", scatter_dimension=3, tiled=True
    ).astype(jnp.float32)
    local_sq = jnp.sum(average * average, axis=(2, 3))
    total_sq = lax.psum(local_sq, ("path", "fsdp"))
    entries = average.shape[2] * average.shape[3] * lax.axis_size("path") * lax.axis_size("fsdp")
    factor = jnp.minimum(1.0, clip_rms / jnp.sqrt(total_sq / entries + epsilon_sq))
    clipped = factor[:, :, None, None] * average
    skipped = (skip_flags > 0)[:, :, None, None]
    momentum_next = jnp.where(skipped, momentum, momentum_coef * momentum + clipped)
    params_next = jnp.where(
        skipped,
        global_params,
        global_params - outer_rate * (clipped + momentum_coef * momentum_next),
    )
    narrow = params_next.astype(jnp.bfloat16)
    outgoing = jnp.where((routes == 1)[:, :, None, None], narrow[None, :, 1], narrow[None, :, 0])
    returned = lax.all_to_all(outgoing, "path", split_axis=0, concat_axis=3, tiled=True)
    return (feedback_next[None], momentum_next, params_next, returned)


def solution(mesh):
    return jax.shard_map(
        on_device,
        mesh=mesh,
        in_specs=(
            P("path", None, "fsdp", None),
            P("path", None, "fsdp", None),
            P(None, None, "fsdp", "path"),
            P(None, None, "fsdp", "path"),
            P(),
            P(),
            P(),
        ),
        out_specs=(
            P("path", None, "fsdp", None),
            P(None, None, "fsdp", "path"),
            P(None, None, "fsdp", "path"),
            P("path", None, "fsdp", None),
        ),
        check_vma=False,
    )
```

profile of v0, /device:TPU:0, one launch (start us, length us, event | category | flops | bytes accessed | tf_op | source)
XLA Modules:
  0.0 136.3 jit_solution(1709357491064695534)
XLA Ops:
  7.2 0.0 reduce-scatter.2.cloned.1.call-start
  7.2 0.8 slice_bitcast_fusion.3
  8.0 0.7 convert_element_type.55
  8.7 0.9 select_reduce_fusion
  9.6 0.7 convert_divide_fusion
  10.3 0.9 dynamic-slice_reduce_fusion
  11.1 0.8 subtract_convert_fusion
  11.9 0.2 dynamic-slice_reduce_fusion.1
  12.1 0.1 fusion.9
  12.2 2.3 %fusion.3 = f32[4,32,4096]{2,1,0:T(8,128)S(1)} fusion(f32[1,4,32,4096]{3,2,1,0:T(8,128)} %param.8, bf16[1,4,32,4096]{3,2,1,0:T(8,128)(2,1)} %param.7, f32[4]{0:T(128)S(1)} %get-tuple-element.13, pred[4]{0:T(512)(128)(4,1)S(1)} %broadcast_compare_fusion.2), kind=kLoop, calls=%fused_computation.8 | loop fusion | flops 3145728 | bytes 5242900 | tf_op jit(solution)/shard_map/convert_element_type | solution.py:27
  14.5 1.7 %multiply_convert_fusion = bf16[4,2,32,4096]{3,2,1,0:T(8,128)(2,1)} fusion(f32[4,32,4096]{2,1,0:T(8,128)S(1)} %fusion.3, f32[4,2]{1,0:T(4,128)S(1)} %fusion.9), kind=kLoop, calls=%fused_computation | loop fusion | flops 2097152 | bytes 4194336 | tf_op jit(solution)/shard_map/convert_element_type | solution.py:32
  16.2 0.0 copy-start.3
  16.2 0.0 copy-start.1
  16.2 0.0 copy-start.2
  16.2 0.0 reduce-scatter.2.cloned.1.call-update
  16.2 0.6 copy-done.3
  16.9 0.1 copy.29
  17.0 38.2 %reduce-scatter.2.cloned.1.call-done = bf16[4,2,32,512]{3,2,1,0:T(8,128)(2,1)} async-done(((bf16[4,2,32,4096]{3,2,1,0:T(8,128)(2,1)}), bf16[4,2,32,512]{3,2,1,0:T(8,128)(2,1)}) %reduce-scatter.2.cloned.1.call-update) | async-done | bytes 262160 | tf_op jit(solution)/shard_map/reduce_scatter | solution.py:31
  55.1 1.1 fusion.8
  56.2 0.1 copy.30
  56.3 37.9 %psum.7 = f32[4,2]{1,0:T(4,128)S(1)} all-reduce(f32[4,2]{1,0:T(4,128)S(1)} %fusion.8), channel_id=1, replica_groups=mesh['path'=8,'fsdp'=4] {'path','fsdp'}, use_global_device_ids=true, to_apply=%region_3.4 | all-reduce | flops 8 | bytes 64 | tf_op jit(solution)/shard_map/psum | solution.py:35
  94.2 0.0 copy-done.1
  94.2 0.0 copy-done.2
  94.2 2.2 %fusion.10 = (bf16[4,2,32,512]{3,2,1,0:T(8,128)(2,1)S(1)}, f32[4,2,32,512]{3,2,1,0:T(8,128)}, f32[4,2,32,512]{3,2,1,0:T(8,128)}) fusion(f32[4,2,32,512]{3,2,1,0:T(8,128)S(1)} %copy-done.1, bf16[4,2,32,512]{3,2,1,0:T(8,128)(2,1)} %reduce-scatter.2.cloned.1.call-done, f32[4,2]{1,0:T(4,128)S(1)} %multiply_minimum_fusion, pred[4,2]{1,0:T(4,128)(4,1)S(1)} %copy.29, ...), kind=kLoop, calls=%fused_computation.34 | loop fusion | flops 1441792 | bytes 2621480 | tf_op jit(solution)/shard_map/convert_element_type | solution.py:46
  96.5 0.0 copy-start
  96.5 1.1 broadcast_select_fusion
  97.6 4.2 %all-to-all-start = ((bf16[8,4,32,512]{3,2,1,0:T(8,128)(2,1)}), bf16[8,4,32,512]{3,2,1,0:T(8,128)(2,1)S(1)}, u32[]{:S(2)}, u32[]{:S(2)}) async-start(bf16[8,4,32,512]{3,2,1,0:T(8,128)(2,1)} %broadcast_select_fusion), calls=%async_computation.1 | async-start | bytes 2097152 | tf_op jit(solution)/shard_map/all_to_all | solution.py:48
  101.8 0.0 copy-done
  101.8 3.1 %multiply_subtract_fusion = f32[1,4,32,4096]{3,2,1,0:T(8,128)} fusion(f32[1,4,32,4096]{3,2,1,0:T(8,128)S(1)} %copy-done, bf16[1,4,32,4096]{3,2,1,0:T(8,128)(2,1)} %param.7, f32[4]{0:T(128)S(1)} %get-tuple-element.13, f32[4]{0:T(128)S(1)} %get-tuple-element.14, pred[4]{0:T(512)(128)(4,1)S(1)} %broadcast_compare_fusion.2), kind=kLoop, calls=%fused_computation.3 | loop fusion | flops 4718592 | bytes 5242916 | tf_op jit(solution)/shard_map/sub | solution.py:26
  104.9 23.5 %all-to-all-done = bf16[8,4,32,512]{3,2,1,0:T(8,128)(2,1)S(1)} async-done(((bf16[8,4,32,512]{3,2,1,0:T(8,128)(2,1)}), bf16[8,4,32,512]{3,2,1,0:T(8,128)(2,1)S(1)}, u32[]{:S(2)}, u32[]{:S(2)}) %all-to-all-start) | async-done | bytes 1048608 | tf_op jit(solution)/shard_map/all_to_all | solution.py:48
  128.4 1.1 copy.32
  (4 shorter events, 0.0 us)
Async XLA Ops:
  7.2 48.0 %reduce-scatter.2.cloned.1.call-start = ((), (), s32[]{:S(2)}) async-start(), calls=%async_computation.2 | async-start | bytes 2359296 | tf_op jit(solution)/shard_map/reduce_scatter | solution.py:31
  16.2 0.7 copy-start.3
  16.2 78.0 %copy-start.1 = (f32[4,2,32,512]{3,2,1,0:T(8,128)S(1)}, f32[4,2,32,512]{3,2,1,0:T(8,128)}, u32[]{:S(2)}) copy-start(f32[4,2,32,512]{3,2,1,0:T(8,128)} %param.9) | copy-start | bytes 1572868
  16.2 78.0 %copy-start.2 = (f32[4,2,32,512]{3,2,1,0:T(8,128)S(1)}, f32[4,2,32,512]{3,2,1,0:T(8,128)}, u32[]{:S(2)}) copy-start(f32[4,2,32,512]{3,2,1,0:T(8,128)} %param.10) | copy-start | bytes 1572868
  96.5 5.4 %copy-start = (f32[1,4,32,4096]{3,2,1,0:T(8,128)S(1)}, f32[1,4,32,4096]{3,2,1,0:T(8,128)}, u32[]{:S(2)}) copy-start(f32[1,4,32,4096]{3,2,1,0:T(8,128)} %param.8) | copy-start | bytes 6291460
  97.6 30.8 %all-to-all-start = ((bf16[8,4,32,512]{3,2,1,0:T(8,128)(2,1)}), bf16[8,4,32,512]{3,2,1,0:T(8,128)(2,1)S(1)}, u32[]{:S(2)}, u32[]{:S(2)}) async-start(bf16[8,4,32,512]{3,2,1,0:T(8,128)(2,1)} %broadcast_select_fusion), calls=%async_computation.1 | async-start | bytes 2097152 | tf_op jit(solution)/shard_map/all_to_all | solution.py:48
Sparse Core Ops, SparseCore 0:
  16.3 38.7 reduce-scatter.1
where the time goes:
time: 137 us; the launch traced here: 136 us
  waiting for transfers between devices  61.7 us (45%)
  blocking collectives  37.9 us (28%)
  other arithmetic  14.6 us (11%)
  between operations  14.1 us (10%)
  starting transfers between devices  4.26 us (3%)
  local copies, waits for them, and re-layouts  3.82 us (3%)
    reduce_scatter x1, waiting for transfers between devices, on_device(): lax.psum_scatter(terms.astype(jnp.bfloat16), 'path', scatter_dimension=3,...  38.2 us
    psum x1, blocking collectives, on_device(): total_sq = lax.psum(local_sq, ('path', 'fsdp'))  37.9 us
    all_to_all x1, waiting for transfers between devices, on_device(): lax.all_to_all(outgoing, 'path', split_axis=0, concat_axis=3, tiled=True)  23.5 us
    all_to_all x1, starting transfers between devices, on_device(): lax.all_to_all(outgoing, 'path', split_axis=0, concat_axis=3, tiled=True)  4.22 us
    sub x1, other arithmetic, on_device(): corrected - own_live[:, None, None] * (sent.astype(jnp.float32) / own_wei...  3.07 us
  transfers between devices with their start and end apart: 2, of which 2 were waited for; matrix products, arithmetic and copies ran while one was open for 2% of the time, Pallas kernels for 0%

commit v1 on v0

--- a/solution.py
+++ b/solution.py
@@ -45,7 +45,15 @@
     )
     narrow = params_next.astype(jnp.bfloat16)
     outgoing = jnp.where((routes == 1)[:, :, None, None], narrow[None, :, 1], narrow[None, :, 0])
-    returned = lax.all_to_all(outgoing, "path", split_axis=0, concat_axis=3, tiled=True)
+
+    def attach_shelves(patch):
+        finding = lax.axis_size("path")
+        a_now = jnp.split(patch, finding, axis=0)
+        piece_now = jnp.stack(a_now)
+        shaped = lax.all_to_all(piece_now, "path", 0, 0)
+        return jnp.concatenate(shaped, axis=3)
+
+    returned = attach_shelves(outgoing)
     return (feedback_next[None], momentum_next, params_next, returned)
 
 

time: 137 us -> 141 us (1.029)
  local copies, waits for them, and re-layouts: 3.82 us -> 9.13 us
    unnamed x8 -> x15, local copies, waits for them, and re-layouts: 0.66 us -> 5.31 us
where the time goes in v1:
time: 141 us
  waiting for transfers between devices  61.7 us (44%)
  blocking collectives  37.9 us (27%)
  between operations  14.1 us (10%)
  other arithmetic  13.7 us (10%)
  local copies, waits for them, and re-layouts  9.13 us (6%)
  starting transfers between devices  4.26 us (3%)
    reduce_scatter x1, waiting for transfers between devices, on_device(): lax.psum_scatter(terms.astype(jnp.bfloat16), 'path', scatter_dimension=3,...  38.2 us
    psum x1, blocking collectives, on_device(): total_sq = lax.psum(local_sq, ('path', 'fsdp'))  37.9 us
    all_to_all x1, waiting for transfers between devices, attach_shelves(): shaped = lax.all_to_all(piece_now, 'path', 0, 0)  23.5 us
    unnamed x15, local copies, waits for them, and re-layouts  5.31 us
    all_to_all x1, starting transfers between devices, attach_shelves(): shaped = lax.all_to_all(piece_now, 'path', 0, 0)  4.22 us
    sub x1, other arithmetic, on_device(): corrected - own_live[:, None, None] * (sent.astype(jnp.float32) / own_wei...  3.07 us
  transfers between devices with their start and end apart: 2, of which 2 were waited for; matrix products, arithmetic and copies ran while one was open for 2% of the time, Pallas kernels for 0%

profile of v1, /device:TPU:0, one launch (start us, length us, event | category | flops | bytes accessed | tf_op | source)
XLA Modules:
  0.0 140.7 jit_solution(3726895523455588675)
XLA Ops:
  7.2 0.0 reduce-scatter.2.cloned.1.call-start
  7.2 0.8 slice_bitcast_fusion.11
  8.0 0.7 convert_element_type.55
  8.7 0.9 select_reduce_fusion
  9.6 0.7 convert_divide_fusion
  10.3 0.9 dynamic-slice_reduce_fusion
  11.1 0.8 subtract_convert_fusion
  11.9 0.2 dynamic-slice_reduce_fusion.1
  12.1 0.1 fusion.17
  12.2 2.3 %fusion.3 = f32[4,32,4096]{2,1,0:T(8,128)S(1)} fusion(f32[1,4,32,4096]{3,2,1,0:T(8,128)} %param.8, bf16[1,4,32,4096]{3,2,1,0:T(8,128)(2,1)} %param.7, f32[4]{0:T(128)S(1)} %get-tuple-element.13, pred[4]{0:T(512)(128)(4,1)S(1)} %broadcast_compare_fusion.2), kind=kLoop, calls=%fused_computation.8 | loop fusion | flops 3145728 | bytes 5242900 | tf_op jit(solution)/shard_map/convert_element_type | solution.py:27
  14.5 1.7 %multiply_convert_fusion = bf16[4,2,32,4096]{3,2,1,0:T(8,128)(2,1)} fusion(f32[4,32,4096]{2,1,0:T(8,128)S(1)} %fusion.3, f32[4,2]{1,0:T(4,128)S(1)} %fusion.17), kind=kLoop, calls=%fused_computation | loop fusion | flops 2097152 | bytes 4194336 | tf_op jit(solution)/shard_map/convert_element_type | solution.py:32
  16.2 0.0 reduce-scatter.2.cloned.1.call-update
  16.2 0.6 copy-done.3
  16.9 0.1 copy.37
  17.0 38.2 %reduce-scatter.2.cloned.1.call-done = bf16[4,2,32,512]{3,2,1,0:T(8,128)(2,1)} async-done(((bf16[4,2,32,4096]{3,2,1,0:T(8,128)(2,1)}), bf16[4,2,32,512]{3,2,1,0:T(8,128)(2,1)}) %reduce-scatter.2.cloned.1.call-update) | async-done | bytes 262160 | tf_op jit(solution)/shard_map/reduce_scatter | solution.py:31
  55.1 1.1 fusion.8
  56.2 0.1 copy.38
  56.3 37.9 %psum.7 = f32[4,2]{1,0:T(4,128)S(1)} all-reduce(f32[4,2]{1,0:T(4,128)S(1)} %fusion.8), channel_id=1, replica_groups=mesh['path'=8,'fsdp'=4] {'path','fsdp'}, use_global_device_ids=true, to_apply=%region_3.4 | all-reduce | flops 8 | bytes 64 | tf_op jit(solution)/shard_map/psum | solution.py:35
  94.2 2.2 %fusion.18 = (bf16[4,2,32,512]{3,2,1,0:T(8,128)(2,1)S(1)}, f32[4,2,32,512]{3,2,1,0:T(8,128)}, f32[4,2,32,512]{3,2,1,0:T(8,128)}) fusion(f32[4,2,32,512]{3,2,1,0:T(8,128)S(1)} %copy-done.1, bf16[4,2,32,512]{3,2,1,0:T(8,128)(2,1)} %reduce-scatter.2.cloned.1.call-done, f32[4,2]{1,0:T(4,128)S(1)} %multiply_minimum_fusion, pred[4,2]{1,0:T(4,128)(4,1)S(1)} %copy.37, ...), kind=kLoop, calls=%fused_computation.50 | loop fusion | flops 1441792 | bytes 2621480 | tf_op jit(solution)/shard_map/convert_element_type | solution.py:46
  96.5 0.1 broadcast_select_fusion
  96.7 0.7 fusion.16
  97.3 0.7 fusion.15
  98.0 0.7 fusion.14
  98.6 0.7 fusion.13
  99.3 0.7 fusion.12
  100.0 0.7 fusion.11
  100.6 0.7 fusion.10
  101.3 0.7 fusion.9
  102.0 4.2 %all-to-all-start = ((bf16[8,1,4,32,512]{4,3,2,1,0:T(8,128)(2,1)}), bf16[8,1,4,32,512]{4,3,2,1,0:T(8,128)(2,1)S(1)}, u32[]{:S(2)}, u32[]{:S(2)}) async-start(bf16[8,1,4,32,512]{4,3,2,1,0:T(8,128)(2,1)} %fusion.9), calls=%async_computation.1 | async-start | bytes 2097152 | tf_op jit(solution)/shard_map/all_to_all | solution.py:53
  106.2 3.1 %multiply_subtract_fusion = f32[1,4,32,4096]{3,2,1,0:T(8,128)} fusion(f32[1,4,32,4096]{3,2,1,0:T(8,128)S(1)} %copy-done, bf16[1,4,32,4096]{3,2,1,0:T(8,128)(2,1)} %param.7, f32[4]{0:T(128)S(1)} %get-tuple-element.13, f32[4]{0:T(128)S(1)} %get-tuple-element.14, pred[4]{0:T(512)(128)(4,1)S(1)} %broadcast_compare_fusion.2), kind=kLoop, calls=%fused_computation.3 | loop fusion | flops 4718592 | bytes 5242916 | tf_op jit(solution)/shard_map/sub | solution.py:26
  109.3 23.5 %all-to-all-done = bf16[8,1,4,32,512]{4,3,2,1,0:T(8,128)(2,1)S(1)} async-done(((bf16[8,1,4,32,512]{4,3,2,1,0:T(8,128)(2,1)}), bf16[8,1,4,32,512]{4,3,2,1,0:T(8,128)(2,1)S(1)}, u32[]{:S(2)}, u32[]{:S(2)}) %all-to-all-start) | async-done | bytes 1048608 | tf_op jit(solution)/shard_map/all_to_all | solution.py:53
  132.8 1.1 copy.40
  (11 shorter events, 0.1 us)
Async XLA Ops:
  7.2 48.0 %reduce-scatter.2.cloned.1.call-start = ((), (), s32[]{:S(2)}) async-start(), calls=%async_computation.2 | async-start | bytes 2359296 | tf_op jit(solution)/shard_map/reduce_scatter | solution.py:31
  16.2 0.7 copy-start.3
  16.2 78.0 %copy-start.1 = (f32[4,2,32,512]{3,2,1,0:T(8,128)S(1)}, f32[4,2,32,512]{3,2,1,0:T(8,128)}, u32[]{:S(2)}) copy-start(f32[4,2,32,512]{3,2,1,0:T(8,128)} %param.9) | copy-start | bytes 1572868
  16.2 78.0 %copy-start.2 = (f32[4,2,32,512]{3,2,1,0:T(8,128)S(1)}, f32[4,2,32,512]{3,2,1,0:T(8,128)}, u32[]{:S(2)}) copy-start(f32[4,2,32,512]{3,2,1,0:T(8,128)} %param.10) | copy-start | bytes 1572868
  96.6 9.6 %copy-start = (f32[1,4,32,4096]{3,2,1,0:T(8,128)S(1)}, f32[1,4,32,4096]{3,2,1,0:T(8,128)}, u32[]{:S(2)}) copy-start(f32[1,4,32,4096]{3,2,1,0:T(8,128)} %param.8) | copy-start | bytes 6291460
  102.0 30.8 %all-to-all-start = ((bf16[8,1,4,32,512]{4,3,2,1,0:T(8,128)(2,1)}), bf16[8,1,4,32,512]{4,3,2,1,0:T(8,128)(2,1)S(1)}, u32[]{:S(2)}, u32[]{:S(2)}) async-start(bf16[8,1,4,32,512]{4,3,2,1,0:T(8,128)(2,1)} %fusion.9), calls=%async_computation.1 | async-start | bytes 2097152 | tf_op jit(solution)/shard_map/all_to_all | solution.py:53
Sparse Core Ops, SparseCore 0:
  16.3 38.7 reduce-scatter.1
